TPU v7x, 512 devices: a whole 4x8x8 slice. The times are simulated.
512 devices in a mesh: dp: 16 (over y_hi, z), blk: 32 (over x, y_lo, core).
Axes of the slice: x: 4, y: 8 (y_hi: 2, y_lo: 4; y = y_hi * 4 + y_lo), z: 8, core: 2. Of those that a mesh axis runs over, the one named last changes fastest.
Arguments:
- queries: bfloat16 [65536, 2048], P(('dp', 'blk')), may hold values from -54 to 54
- keys: bfloat16 [4096, 2048], P(('dp', 'blk')), may hold values from -7 to 7
- memory_values: bfloat16 [4096, 2048], P(('dp', 'blk')), may hold values from -6 to 6
- block_mask: int32 [1024, 32], P(('dp', 'blk')), may hold values from 0 to 1, as said below
- head_gate: float32 [16], replicated, may hold values from 0.5 to 2
- out_grad: bfloat16 [65536, 2048], P(('dp', 'blk')), may hold values from -6 to 6
Outputs:
- attended: bfloat16 [65536, 2048], P(('dp', 'blk'))
- query_gradient: bfloat16 [65536, 2048], P(('dp', 'blk'))
- key_gradient: float32 [4096, 2048], P(('dp', 'blk'))
- value_gradient: float32 [4096, 2048], P(('dp', 'blk'))
- gate_grad: float32 [16], replicated
Inputs may be any that keep to these rules, and one draw needn't show every extreme that they name: `block_mask`: every row has at least one 1. Column b stands for the memory rows of block b of the row's batch.
All inputs are finite; a program needn't handle non-finite values.
Results may differ from a plain program's by a relative error of at most 0.02.
Values may be sent and summed in bfloat16 or wider, within the bound.
A program may use at most 64 MiB of HBM per device.

v0:
```python
import math

import jax
import jax.numpy as jnp
from jax import lax
from jax.sharding import PartitionSpec as P

QBLK = 64


def on_device(queries, keys, memory_values, block_mask, head_gate, out_grad):
    query_count = queries.shape[0]
    full_width = queries.shape[1]
    head_count = head_gate.shape[0]
    head_size = full_width // head_count
    memory_count = keys.shape[0]
    score_scale = 1.0 / math.sqrt(head_size)
    keys_all, values_all = (
        lax.all_gather(keys, "blk", axis=0, tiled=True),
        lax.all_gather(memory_values, "blk", axis=0, tiled=True),
    )
    allowed = jnp.repeat(jnp.repeat(block_mask, QBLK, axis=0), memory_count, axis=1) > 0
    split_query_heads = queries.reshape(query_count, head_count, head_size)
    split_key_heads = keys_all.reshape(-1, head_count, head_size)
    split_value_heads = values_all.reshape(-1, head_count, head_size)
    logit_scores = (
        jnp.einsum(
            "bes,fes->ebf", split_query_heads, split_key_heads, preferred_element_type=jnp.float32
        )
        * score_scale
    )
    logit_scores = jnp.where(allowed[None], logit_scores, jnp.float32(-1e30))
    largest = jnp.max(logit_scores, axis=2, keepdims=True)
    raised = jnp.exp(logit_scores - largest)
    totals = jnp.sum(raised, axis=2, keepdims=True)
    probs = raised / totals
    narrow_probabilities = probs.astype(jnp.bfloat16)
    output_heads = jnp.einsum(
        "bzf,fbs->zbs", narrow_probabilities, split_value_heads, preferred_element_type=jnp.float32
    )
    attended = (
        (head_gate[None, :, None] * output_heads)
        .astype(jnp.bfloat16)
        .reshape(query_count, full_width)
    )
    grad_heads = out_grad.reshape(query_count, head_count, head_size).astype(jnp.float32)
    gate_part = jnp.sum(grad_heads * output_heads, axis=(0, 2))
    scaled_grad = head_gate[None, :, None] * grad_heads
    narrow_scaled_scores = scaled_grad.astype(jnp.bfloat16)
    deltas = jnp.sum(scaled_grad * output_heads, axis=2)
    back_keys, back_values = (
        lax.all_gather(keys, "blk", axis=0, tiled=True),
        lax.all_gather(memory_values, "blk", axis=0, tiled=True),
    )
    returned_key_heads = back_keys.reshape(-1, head_count, head_size)
    returned_value_heads = back_values.reshape(-1, head_count, head_size)
    probability_gradient = jnp.einsum(
        "bes,fes->ebf",
        narrow_scaled_scores,
        returned_value_heads,
        preferred_element_type=jnp.float32,
    )
    score_grads = probs * (probability_gradient - jnp.transpose(deltas)[:, :, None]) * score_scale
    narrow_scores = score_grads.astype(jnp.bfloat16)
    query_gradient = jnp.einsum(
        "bzf,fbs->zbs", narrow_scores, returned_key_heads, preferred_element_type=jnp.float32
    )
    query_gradient = query_gradient.astype(jnp.bfloat16).reshape(query_count, full_width)
    value_term = jnp.einsum(
        "yor,oyt->ryt",
        narrow_probabilities,
        narrow_scaled_scores,
        preferred_element_type=jnp.float32,
    )
    key_term = jnp.einsum(
        "yor,oyt->ryt", narrow_scores, split_query_heads, preferred_element_type=jnp.float32
    )
    memory_grads = lax.psum_scatter(
        jnp.concatenate(
            [
                key_term.reshape(memory_count * lax.axis_size("blk"), full_width),
                value_term.reshape(memory_count * lax.axis_size("blk"), full_width),
            ],
            axis=1,
        ).astype(jnp.bfloat16),
        "blk",
        scatter_dimension=0,
        tiled=True,
    ).astype(jnp.float32)
    key_gradient = memory_grads[:, :full_width]
    value_gradient = memory_grads[:, full_width:]
    gate_total = lax.psum(gate_part, ("dp", "blk"))
    token_total = query_count * lax.axis_size("dp") * lax.axis_size("blk")
    gate_grad = gate_total / math.sqrt(token_total * head_size)
    return (attended, query_gradient, key_gradient, value_gradient, gate_grad)


def solution(mesh):
    placed = (
        P(("dp", "blk"), None),
        P(("dp", "blk"), None),
        P(("dp", "blk"), None),
        P(("dp", "blk"), None),
        P(),
        P(("dp", "blk"), None),
    )
    return jax.shard_map(
        on_device,
        mesh=mesh,
        in_specs=placed,
        out_specs=(
            P(("dp", "blk"), None),
            P(("dp", "blk"), None),
            P(("dp", "blk"), None),
            P(("dp", "blk"), None),
            P(),
        ),
        check_vma=False,
    )
```

profile of v0, /device:TPU:1, one launch (start us, length us, event | category | flops | bytes accessed | tf_op | source)
XLA Modules:
  0.0 308.7 jit_solution(342290486451467460)
XLA Ops:
  7.2 0.7 all-gather.3.cloned.1.call-update
  7.9 0.7 all-gather.5.cloned.1.call-update
  8.7 0.7 broadcast_compare_fusion
  9.8 1.3 copy.67
  11.2 1.4 copy.56
  12.6 64.7 %all-gather.3.cloned.1.call-done = bf16[256,2048]{1,0:T(8,128)(2,1)} async-done(((bf16[8,2048]{1,0:T(8,128)(2,1)}), bf16[256,2048]{1,0:T(8,128)(2,1)}) %all-gather.3.cloned.1.call-update) | async-done | bytes 1048592 | tf_op jit(solution)/shard_map/all_gather | solution.py:19
  77.3 1.5 copy.52
  78.8 2.1 fusion.13
  80.9 3.1 %convolution_convert_fusion.1 = bf16[16,128,256]{2,1,0:T(8,128)(2,1)} fusion(f32[16]{0:T(128)S(1)} %copy-done.5, f32[128,2048]{0,1:T(8,128)S(1)} %copy.56, f32[16,128,256]{2,1,0:T(8,128)} %get-tuple-element.31, f32[16,128]{1,0:T(8,128)S(1)} %get-tuple-element.30), kind=kOutput, calls=%fused_computation.7 | convolution fusion | flops 136314880 | bytes 4202560 | tf_op jit(solution)/shard_map/yor,oyt->ryt/dot_general | solution.py:69
  84.0 55.9 %all-gather.5.cloned.1.call-done = bf16[256,2048]{1,0:T(8,128)(2,1)} async-done(((bf16[8,2048]{1,0:T(8,128)(2,1)}), bf16[256,2048]{1,0:T(8,128)(2,1)}) %all-gather.5.cloned.1.call-update) | async-done | bytes 1048592 | tf_op jit(solution)/shard_map/all_gather | solution.py:20
  139.9 1.5 copy.55
  141.4 3.5 %multiply_reduce_fusion = (f32[16]{0:T(128)S(1)}, f32[128,16]{0,1:T(8,128)S(1)}, bf16[128,16,128]{0,2,1:T(8,128)(2,1)}) fusion(f32[128,16,128]{0,2,1:T(8,128)S(1)} %bitcast.39, f32[128,2048]{0,1:T(8,128)S(1)} %copy.56, f32[16]{0:T(128)S(1)} %copy-done.5, bf16[256,16,128]{0,2,1:T(8,128)(2,1)S(1)} %bitcast.41, f32[16,128,256]{2,1,0:T(8,128)} %get-tuple-element.31, ...), kind=kOutput, calls=%fused_computation.10 | convolution fusion | flops 137099248 | bytes 5783680 | tf_op jit(solution)/shard_map/bzf,fbs->zbs/dot_general | solution.py:38
  144.9 2.3 multiply_convert_fusion
  147.2 0.4 convolution_convert_fusion
  147.7 1.4 copy.60
  149.1 2.4 copy.61
  151.5 2.7 pad_maximum_fusion
  154.2 100.0 %psum.7 = f32[16]{0:T(128)S(1)} all-reduce(f32[16]{0:T(128)S(1)} %get-tuple-element.25), channel_id=1, replica_groups=mesh['dp'=16,'blk'=32] {'dp','blk'}, use_global_device_ids=true, to_apply=%region_5.6 | all-reduce | flops 16 | bytes 128 | tf_op jit(solution)/shard_map/psum | solution.py:92
  254.2 0.4 convolution_convert_fusion.2
  254.7 1.0 copy.63
  255.7 1.0 copy.62
  256.7 0.5 broadcast_multiply_fusion
  257.2 43.5 %reduce-scatter.2.cloned.1.call-done = bf16[8,4096]{1,0:T(8,128)(2,1)} async-done(((bf16[256,4096]{1,0:T(8,128)(2,1)}), bf16[8,4096]{1,0:T(8,128)(2,1)}) %reduce-scatter.2.cloned.1.call-update) | async-done | bytes 65552 | tf_op jit(solution)/shard_map/reduce_scatter | solution.py:78
  300.7 1.4 fusion.12
  (23 shorter events, 0.6 us)
Async XLA Ops:
  7.2 70.2 %all-gather.3.cloned.1.call-start = ((), (), s32[]{:S(2)}) async-start(), calls=%async_computation.1 | async-start | bytes 1081344 | tf_op jit(solution)/shard_map/all_gather | solution.py:19
  7.9 132.0 %all-gather.5.cloned.1.call-start = ((), (), s32[]{:S(2)}) async-start(), calls=%async_computation.2 | async-start | bytes 1081344 | tf_op jit(solution)/shard_map/all_gather | solution.py:20
  8.6 292.1 %reduce-scatter.2.cloned.1.call-start = ((), (), s32[]{:S(2)}) async-start(), calls=%async_computation.3 | async-start | bytes 2162688 | tf_op jit(solution)/shard_map/reduce_scatter | solution.py:78
  11.2 69.8 %copy-start.1 = (bf16[128,2048]{0,1:T(8,128)(2,1)}, bf16[128,2048]{0,1:T(8,128)(2,1)S(1)}, u32[]{:S(2)}) copy-start(bf16[128,2048]{0,1:T(8,128)(2,1)S(1)} %copy.67) | copy-start | bytes 1572868
  78.8 2.1 copy-start.5
  141.4 3.5 %copy-start.3 = (bf16[256,2048]{0,1:T(8,128)(2,1)}, bf16[256,2048]{0,1:T(8,128)(2,1)S(1)}, u32[]{:S(2)}) copy-start(bf16[256,2048]{0,1:T(8,128)(2,1)S(1)} %copy.55) | copy-start | bytes 3145732
  141.4 3.5 %copy-start.6 = (f32[16,128,256]{2,1,0:T(8,128)S(1)}, f32[16,128,256]{2,1,0:T(8,128)}, u32[]{:S(2)}) copy-start(f32[16,128,256]{2,1,0:T(8,128)} %get-tuple-element.31) | copy-start | bytes 6291460
  144.9 2.4 copy-start.2
  149.1 2.4 copy-start
  154.2 101.4 %copy-start.4 = (bf16[128,16,128]{0,2,1:T(8,128)(2,1)S(1)}, bf16[128,16,128]{0,2,1:T(8,128)(2,1)}, u32[]{:S(2)}) copy-start(bf16[128,16,128]{0,2,1:T(8,128)(2,1)} %get-tuple-element.27) | copy-start | bytes 1572868
Sparse Core Ops, SparseCore 0:
  10.1 67.1 all-gather.2
  79.5 60.3 all-gather.4
  154.4 146.3 reduce-scatter.1
where the time goes:
time: 312 us; the launch traced here: 309 us
  waiting for transfers between devices  165 us (53%)
  blocking collectives  100 us (32%)
  between operations  13.9 us (4%)
  local copies, waits for them, and re-layouts  13.4 us (4%)
  matrix products  11.9 us (4%)
  other arithmetic  3.94 us (1%)
    psum x1, blocking collectives, on_device(): gate_total = lax.psum(gate_part, ('dp', 'blk'))  100 us
    all_gather x1, waiting for transfers between devices, on_device(): lax.all_gather(keys, 'blk', axis=0, tiled=True)  64.7 us
    all_gather x1, waiting for transfers between devices, on_device(): lax.all_gather(memory_values, 'blk', axis=0, tiled=True)  55.9 us
    reduce_scatter x1, waiting for transfers between devices, on_device(): lax.psum_scatter(jnp.concatenate([key_term.reshape(memory_count * lax.axi...  43.5 us
  transfers between devices with their start and end apart: 3, of which 3 were waited for; matrix products, arithmetic and copies ran while one was open for 4% of the time, Pallas kernels for 0%

commit v1 on v0

v1 whole, which is shorter than its diff:
```python
import math

import jax
import jax.numpy as jnp
from jax import lax
from jax.experimental import pallas as pl
from jax.experimental.pallas import tpu as pltpu
from jax.sharding import PartitionSpec as P

MESH = pl.DeviceIdType.MESH
HEADS, HEAD_DIM, QBLK = 16, 128, 64
TQ, TM, FEAT = 128, 8, 2048
NX, NY, NZ, NYL = 4, 8, 8, 4
HALF = FEAT // 2
CHUNKS = 2
CH_HEADS = HEADS // 2 // CHUNKS
CW = CH_HEADS * HEAD_DIM
CHIPS = NX * NYL
ROWS = 2 * TM
MEM = CHIPS * ROWS
NQ = 2 * TQ
SEMS = 80
BF, F32 = jnp.bfloat16, jnp.float32


def nt(a, b):
    return lax.dot_general(a, b, (((1,), (1,)), ((), ())), preferred_element_type=F32)


def tn(a, b):
    return lax.dot_general(a, b, (((0,), (0,)), ((), ())), preferred_element_type=F32)


def nn(a, b):
    return lax.dot_general(a, b, (((1,), (0,)), ((), ())), preferred_element_type=F32)


def kernel(
    q_ref, k_ref, v_ref, mask_ref, gate_ref, og_ref,
    att_out, qg_out, kg_out, vg_out, gg_out,
    kx, vx, qa, oa, mb, bias, gath, att, qg, term, rxa, rxn, ysum, yrx, fin, gsl, send, recv, local,
):
    dp, blk = lax.axis_index("dp"), lax.axis_index("blk")
    y_hi, z = dp // NZ, dp % NZ
    x, y_lo, c = blk // (2 * NYL), (blk // 2) % NYL, blk % 2
    y = y_hi * NYL + y_lo
    me = x * NYL + y_lo

    def device(x=x, y=y, z=z, c=c):
        return (y // NYL * NZ + z, x * (2 * NYL) + (y % NYL) * 2 + c)

    partner = device(c=1 - c)
    right, left = device(x=(x + 1) % NX), device(x=(x + NX - 1) % NX)
    y_near = [device(y=y_hi * NYL + (y_lo + d) % NYL) for d in range(1, NYL)]
    gate_peers = [
        [device(x=(x + d) % NX) for d in range(1, NX)],
        [device(y=(y + d) % NY) for d in range(1, NY)],
        [device(z=(z + d) % NZ) for d in range(1, NZ)],
        [partner],
    ]

    count = [0, 0]
    sent, stayed = [], []

    def remote(src, dst, to):
        i = count[0]
        count[0] += 1
        copy = pltpu.make_async_remote_copy(
            src_ref=src, dst_ref=dst, send_sem=send.at[i], recv_sem=recv.at[i],
            device_id=to, device_id_type=MESH,
        )
        copy.start()
        sent.append(copy)
        return copy

    def stay(src, dst):
        i = count[1]
        count[1] += 1
        copy = pltpu.make_async_copy(src, dst, local.at[i])
        copy.start()
        return copy

    mine = pl.ds(pl.multiple_of(c * HALF, HALF), HALF)
    other = pl.ds(pl.multiple_of((1 - c) * HALF, HALF), HALF)

    own_kv = [stay(k_ref.at[:, mine], kx.at[c]), stay(v_ref.at[:, mine], vx.at[c])]
    own_q = [stay(q_ref.at[:, mine], qa.at[0]), stay(og_ref.at[:, mine], oa.at[0])]
    mb[0] = jnp.zeros((8, 128), F32)
    mb[0, 0:2, 0 : 2 * CHIPS] = mask_ref[...].astype(F32)

    barrier = pltpu.get_barrier_semaphore()
    peers = [to for stage in gate_peers for to in stage]
    for to in peers:
        pl.semaphore_signal(barrier, inc=1, device_id=to, device_id_type=MESH)
    pl.semaphore_wait(barrier, len(peers))

    kv_in = [
        remote(k_ref.at[:, other], kx.at[c], partner),
        remote(v_ref.at[:, other], vx.at[c], partner),
    ]
    mask_in = remote(mb.at[0], mb.at[1], partner)
    q_in = [
        remote(q_ref.at[:, other], qa.at[1], partner),
        remote(og_ref.at[:, other], oa.at[1], partner),
    ]

    for copy in own_kv:
        copy.wait()
    for copy in kv_in:
        copy.wait_recv()
    k_rows = kx[...].astype(F32).reshape(ROWS, HALF).astype(BF)
    v_rows = vx[...].astype(F32).reshape(ROWS, HALF).astype(BF)
    for j in range(CHUNKS):
        gath[j, me, :, 0:CW] = k_rows[:, j * CW : (j + 1) * CW]
        gath[j, me, :, CW : 2 * CW] = v_rows[:, j * CW : (j + 1) * CW]

    y_in = [
        [remote(gath.at[j, me], gath.at[j, me], to) for to in y_near] for j in range(CHUNKS)
    ]

    mask_in.wait_recv()
    rows = lax.broadcasted_iota(jnp.int32, (MEM, 128), 0) // TM
    lanes = lax.broadcasted_iota(jnp.int32, (MEM, 128), 1)
    pick = jnp.where(rows == lanes, 1.0, 0.0).astype(F32)
    spread = jnp.concatenate(
        [jnp.broadcast_to(mb[s, b : b + 1, :], (QBLK, 128)) for s in range(2) for b in range(2)],
        axis=0,
    )
    bias[...] = (nt(pick.astype(BF), spread.astype(BF)) - 1.0) * 1e30

    x_of = lambda d: (x + d) % NX
    x_in = []
    for j in range(CHUNKS):
        for copy in y_in[j]:
            copy.wait_recv()
        block = gath.at[j, pl.ds(x * NYL, NYL)]
        x_in.append([remote(block, block, right), remote(block, block, left)])
    far_in = []
    for j in range(CHUNKS):
        x_in[j][0].wait_recv()
        part = gath.at[j, pl.ds(x_of(3) * NYL, 2)]
        first = remote(part, part, right)
        x_in[j][1].wait_recv()
        part = gath.at[j, pl.ds(x_of(1) * NYL + 2, 2)]
        far_in.append([first, remote(part, part, left)])

    for copy in own_q:
        copy.wait()
    for copy in q_in:
        copy.wait_recv()

    scale = 1.0 / math.sqrt(HEAD_DIM)
    lane = lax.broadcasted_iota(jnp.int32, (8, 128), 1)
    gate_row = jnp.zeros((8, 128), F32)
    rx1 = []
    for j in range(CHUNKS):
        for copy in far_in[j]:
            copy.wait_recv()
        for h in range(CH_HEADS):
            head = j * CH_HEADS + h
            cols = slice(head * HEAD_DIM, (head + 1) * HEAD_DIM)
            kc = slice(h * HEAD_DIM, (h + 1) * HEAD_DIM)
            vc = slice(CW + h * HEAD_DIM, CW + (h + 1) * HEAD_DIM)
            g = gate_ref[c * (HEADS // 2) + head]
            qh = qa[:, :, cols].reshape(NQ, HEAD_DIM)
            oh = oa[:, :, cols].reshape(NQ, HEAD_DIM)
            kh = gath[j, :, :, kc].reshape(MEM, HEAD_DIM)
            vh = gath[j, :, :, vc].reshape(MEM, HEAD_DIM)
            s = nt(kh, qh) * (scale * math.log2(math.e)) + bias[...]
            e = jnp.exp2(s - jnp.max(s, axis=0, keepdims=True))
            p = e * (1.0 / jnp.sum(e, axis=0, keepdims=True))
            low = p.astype(BF)
            dp_ = nt(vh, oh)
            delta = jnp.sum(low.astype(F32) * dp_, axis=0, keepdims=True)
            ds = (p * (dp_ - delta) * (g * scale)).astype(BF)
            term[j, :, :, kc] = nn(ds, qh).astype(BF).reshape(CHIPS, ROWS, HEAD_DIM)
            term[j, :, :, vc] = (nn(low, oh) * g).astype(BF).reshape(CHIPS, ROWS, HEAD_DIM)
            att[:, :, cols] = (tn(low, vh) * g).astype(BF).reshape(2, TQ, HEAD_DIM)
            qg[:, :, cols] = tn(ds, kh).astype(BF).reshape(2, TQ, HEAD_DIM)
            total = jnp.sum(delta, axis=1, keepdims=True)
            gate_row = gate_row + jnp.where(lane == c * (HEADS // 2) + head, total, 0.0)
        rx1.append([
            remote(term.at[j, pl.ds(x_of(2) * NYL, 2)], rxa.at[j, 0], right),
            remote(term.at[j, pl.ds(x_of(2) * NYL + 2, 2)], rxa.at[j, 1], left),
        ])

    rx2 = []

    def reduce_x(j):
        rx1[j][0].wait_recv()
        to = pl.ds(x_of(1) * NYL, 2)
        term[j, to] = (term[j, to].astype(F32) + rxa[j, 0].astype(F32)).astype(BF)
        first = remote(term.at[j, pl.ds(x_of(1) * NYL, NYL)], rxn.at[j, 0], right)
        rx1[j][1].wait_recv()
        to = pl.ds(x_of(3) * NYL + 2, 2)
        term[j, to] = (term[j, to].astype(F32) + rxa[j, 1].astype(F32)).astype(BF)
        rx2.append([first, remote(term.at[j, pl.ds(x_of(3) * NYL, NYL)], rxn.at[j, 1], left)])

    gate_slots = [(0, NX, x), (NX, NY, y), (NX + NY, NZ, z), (NX + NY + NZ, 2, c)]
    gate_in = []

    def gate_send(stage, row):
        base, _, at = gate_slots[stage]
        gsl[base + at] = row
        for to in gate_peers[stage]:
            gate_in.append(remote(gsl.at[base + at], gsl.at[base + at], to))

    def gate_take(stage):
        base, size, _ = gate_slots[stage]
        for copy in gate_in:
            copy.wait_recv()
        gate_in.clear()
        row = gsl[base]
        for i in range(1, size):
            row = row + gsl[base + i]
        return row

    gate_send(0, gate_row)
    reduce_x(0)
    ends = []

    def put(src, out, j):
        lo = pl.ds(pl.multiple_of(c * HALF + j * CW, CW), CW)
        part = slice(j * CW, (j + 1) * CW)
        ends.append(remote(src.at[1, :, part], out.at[:, lo], partner))
        stayed.append(stay(src.at[0, :, part], out.at[:, lo]))

    reduce_x(1)
    for j in range(CHUNKS):
        put(att, att_out, j)
        put(qg, qg_out, j)
    gate_send(1, gate_take(0))

    ry = []
    for j in range(CHUNKS):
        for copy in rx2[j]:
            copy.wait_recv()
        own = term[j, pl.ds(x * NYL, NYL)].astype(F32)
        ysum[j] = (own + rxn[j, 0].astype(F32) + rxn[j, 1].astype(F32)).astype(BF)
        ry.append([
            remote(ysum.at[j, (y_lo + d) % NYL], yrx.at[j, d - 1], y_near[d - 1])
            for d in range(1, NYL)
        ])
        if j == 0:
            gate_send(2, gate_take(1))

    for j in range(CHUNKS):
        for copy in ry[j]:
            copy.wait_recv()
        whole = ysum[j, y_lo].astype(F32)
        for d in range(NYL - 1):
            whole = whole + yrx[j, d].astype(F32)
        fin[j] = whole.reshape(2, TM, 2 * CW)
        lo = pl.ds(pl.multiple_of(c * HALF + j * CW, CW), CW)
        for out, part in ((kg_out, slice(0, CW)), (vg_out, slice(CW, 2 * CW))):
            ends.append(remote(fin.at[j, 1 - c, :, part], out.at[:, lo], partner))
            stayed.append(stay(fin.at[j, c, :, part], out.at[:, lo]))

    gate_send(3, gate_take(2))
    row = gate_take(3)
    gg_out[...] = row * (1.0 / math.sqrt(TQ * 512 * HEAD_DIM))

    for copy in ends:
        copy.wait_recv()
    for copy in stayed:
        copy.wait()
    for copy in sent:
        copy.wait_send()


def on_device(queries, keys, memory_values, block_mask, head_gate, out_grad):
    anywhere = pl.BlockSpec(memory_space=pl.ANY)
    vmem = pl.BlockSpec(memory_space=pltpu.VMEM)
    smem = pl.BlockSpec(memory_space=pltpu.SMEM)
    attended, query_gradient, key_gradient, value_gradient, gate = pl.pallas_call(
        kernel,
        out_shape=(
            jax.ShapeDtypeStruct((TQ, FEAT), BF),
            jax.ShapeDtypeStruct((TQ, FEAT), BF),
            jax.ShapeDtypeStruct((TM, FEAT), F32),
            jax.ShapeDtypeStruct((TM, FEAT), F32),
            jax.ShapeDtypeStruct((8, 128), F32),
        ),
        in_specs=[anywhere, anywhere, anywhere, vmem, smem, anywhere],
        out_specs=(anywhere, anywhere, anywhere, anywhere, vmem),
        scratch_shapes=[
            pltpu.VMEM((2, TM, HALF), BF),
            pltpu.VMEM((2, TM, HALF), BF),
            pltpu.VMEM((2, TQ, HALF), BF),
            pltpu.VMEM((2, TQ, HALF), BF),
            pltpu.VMEM((2, 8, 128), F32),
            pltpu.VMEM((MEM, NQ), F32),
            pltpu.VMEM((CHUNKS, CHIPS, ROWS, 2 * CW), BF),
            pltpu.VMEM((2, TQ, HALF), BF),
            pltpu.VMEM((2, TQ, HALF), BF),
            pltpu.VMEM((CHUNKS, CHIPS, ROWS, 2 * CW), BF),
            pltpu.VMEM((CHUNKS, 2, 2, ROWS, 2 * CW), BF),
            pltpu.VMEM((CHUNKS, 2, NYL, ROWS, 2 * CW), BF),
            pltpu.VMEM((CHUNKS, NYL, ROWS, 2 * CW), BF),
            pltpu.VMEM((CHUNKS, NYL - 1, ROWS, 2 * CW), BF),
            pltpu.VMEM((CHUNKS, 2, TM, 2 * CW), F32),
            pltpu.VMEM((NX + NY + NZ + 2, 8, 128), F32),
            pltpu.SemaphoreType.DMA((SEMS,)),
            pltpu.SemaphoreType.DMA((SEMS,)),
            pltpu.SemaphoreType.DMA((16,)),
        ],
        compiler_params=pltpu.CompilerParams(
            collective_id=0, has_side_effects=True, vmem_limit_bytes=40 * 1024 * 1024
        ),
    )(queries, keys, memory_values, block_mask, head_gate, out_grad)
    return attended, query_gradient, key_gradient, value_gradient, gate[0, :HEADS]


def solution(mesh):
    placed = P(("dp", "blk"), None)
    return jax.shard_map(
        on_device,
        mesh=mesh,
        in_specs=(placed, placed, placed, placed, P(), placed),
        out_specs=(placed, placed, placed, placed, P()),
        check_vma=False,
    )
```

time: 312 us -> 62.8 us (0.20)
  waiting for transfers between devices: 165 us -> 0 us
  blocking collectives: 100 us -> 0 us
  Pallas kernels: 0 us -> 53.5 us
  between operations: 13.9 us -> 0.66 us
  matrix products: 11.9 us -> 0 us
  local copies, waits for them, and re-layouts: 13.4 us -> 8.28 us
  other arithmetic: 3.94 us -> 0 us
    all_gather x2 -> x0, waiting for transfers between devices: 121 us -> none  [the longest x1 64.7 us: on_device(): lax.all_gather(keys, 'blk', axis=0, tiled=True)]
    psum x1 -> x0, blocking collectives: 100 us -> none  [on_device(): gate_total = lax.psum(gate_part, ('dp', 'blk'))]
    pallas_call x0 -> x1, Pallas kernels: none -> 53.5 us  [on_device(): pl.pallas_call(kernel, out_shape=(jax.ShapeDtypeStruct((TQ, FEAT), BF), j...]
    reduce_scatter x1 -> x0, waiting for transfers between devices: 43.5 us -> none  [on_device(): lax.psum_scatter(jnp.concatenate([key_term.reshape(memory_count * lax.axi...]
    dot_general x5 -> x0, matrix products: 9.79 us -> none  [the longest x1 3.47 us: on_device(): jnp.einsum('bzf,fbs->zbs', narrow_probabilities, split_value_heads, prefe...]
    unnamed x16, local copies, waits for them, and re-layouts: 2.05 us -> 7.77 us
    reshape x3 -> x0, local copies, waits for them, and re-layouts: 5.09 us -> none  [the longest x1 2.36 us: on_device(): value_term.reshape(memory_count * lax.axis_size('blk'), full_width)]
  transfers between devices with their start and end apart: 3 -> 0, of which waited for: 3 -> 0; matrix products, arithmetic and copies ran while one was open for 4% -> 0% of each run, Pallas kernels for 0% -> 0%
where the time goes in v1:
time: 62.8 us; the launch traced here: 62.4 us
  Pallas kernels  53.5 us (85%)
  local copies, waits for them, and re-layouts  8.28 us (13%)
  between operations  0.66 us (1%)
    pallas_call x1, Pallas kernels, on_device(): pl.pallas_call(kernel, out_shape=(jax.ShapeDtypeStruct((TQ, FEAT), BF), j...  53.5 us
    unnamed x16, local copies, waits for them, and re-layouts  7.77 us

profile of v1, /device:TPU:1, one launch (start us, length us, event | category | flops | bytes accessed | tf_op | source)
XLA Modules:
  0.0 62.4 jit_solution(3229041565525243446)
XLA Ops:
  0.6 0.0 copy-start
  0.6 1.0 %copy-done = bf16[128,2048]{1,0:T(8,128)(2,1)S(1)} copy-done((bf16[128,2048]{1,0:T(8,128)(2,1)S(1)}, bf16[128,2048]{1,0:T(8,128)(2,1)}, u32[]{:S(2)}) %copy-start) | copy-done | bytes 524312
  1.7 0.0 copy-start.1
  1.7 1.0 %copy-done.1 = bf16[128,2048]{1,0:T(8,128)(2,1)S(1)} copy-done((bf16[128,2048]{1,0:T(8,128)(2,1)S(1)}, bf16[128,2048]{1,0:T(8,128)(2,1)}, u32[]{:S(2)}) %copy-start.1) | copy-done | bytes 524312
  2.7 0.0 copy-start.2
  2.7 0.8 %copy-done.2 = bf16[8,2048]{1,0:T(8,128)(2,1)S(1)} copy-done((bf16[8,2048]{1,0:T(8,128)(2,1)S(1)}, bf16[8,2048]{1,0:T(8,128)(2,1)}, u32[]{:S(2)}) %copy-start.2) | copy-done | bytes 32792
  3.5 0.0 copy-start.3
  3.5 0.8 %copy-done.3 = bf16[8,2048]{1,0:T(8,128)(2,1)S(1)} copy-done((bf16[8,2048]{1,0:T(8,128)(2,1)S(1)}, bf16[8,2048]{1,0:T(8,128)(2,1)}, u32[]{:S(2)}) %copy-start.3) | copy-done | bytes 32792
  4.2 0.0 copy-start.4
  4.2 0.7 %copy-done.4 = s32[2,32]{1,0:T(2,128)S(1)} copy-done((s32[2,32]{1,0:T(2,128)S(1)}, s32[2,32]{1,0:T(2,128)}, u32[]{:S(2)}) %copy-start.4) | copy-done | bytes 280
  4.9 0.0 copy-start.5
  4.9 0.7 %copy-done.5 = f32[16]{0:T(128)S(1)} copy-done((f32[16]{0:T(128)S(1)}, f32[16]{0:T(128)}, u32[]{:S(2)}) %copy-start.5) | copy-done | bytes 88
  5.6 53.5 %shard_map.101 = (bf16[128,2048]{1,0:T(8,128)(2,1)S(1)}, bf16[128,2048]{1,0:T(8,128)(2,1)S(1)}, f32[8,2048]{1,0:T(8,128)S(1)}, f32[8,2048]{1,0:T(8,128)S(1)}, f32[8,128]{1,0:T(8,128)S(1)}) custom-call(bf16[128,2048]{1,0:T(8,128)(2,1)S(1)} %copy-done, bf16[8,2048]{1,0:T(8,128)(2,1)S(1)} %copy-done.2, bf16[8,2048]{1,0:T(8,128)(2,1)S(1)} %copy-done.3, ...), custom_call_target="tpu_custom_call" | custom-call | tf_op jit(solution)/shard_map/pallas_call | solution.py:275
  59.0 0.5 slice_bitcast_fusion
  59.6 0.8 %copy.15 = bf16[128,2048]{1,0:T(8,128)(2,1)} copy(bf16[128,2048]{1,0:T(8,128)(2,1)S(1)} %get-tuple-element.20) | data formatting | bytes 1048576
  60.3 0.8 %copy.16 = bf16[128,2048]{1,0:T(8,128)(2,1)} copy(bf16[128,2048]{1,0:T(8,128)(2,1)S(1)} %get-tuple-element.21) | data formatting | bytes 1048576
  61.1 0.6 %copy.17 = f32[8,2048]{1,0:T(8,128)} copy(f32[8,2048]{1,0:T(8,128)S(1)} %get-tuple-element.22) | data formatting | bytes 131072
  61.8 0.6 %copy.18 = f32[8,2048]{1,0:T(8,128)} copy(f32[8,2048]{1,0:T(8,128)S(1)} %get-tuple-element.23) | data formatting | bytes 131072
Async XLA Ops:
  0.6 1.0 %copy-start = (bf16[128,2048]{1,0:T(8,128)(2,1)S(1)}, bf16[128,2048]{1,0:T(8,128)(2,1)}, u32[]{:S(2)}) copy-start(bf16[128,2048]{1,0:T(8,128)(2,1)} %q_ref.1) | copy-start | bytes 1572868
  1.7 1.0 %copy-start.1 = (bf16[128,2048]{1,0:T(8,128)(2,1)S(1)}, bf16[128,2048]{1,0:T(8,128)(2,1)}, u32[]{:S(2)}) copy-start(bf16[128,2048]{1,0:T(8,128)(2,1)} %og_ref.1) | copy-start | bytes 1572868
  2.7 0.8 %copy-start.2 = (bf16[8,2048]{1,0:T(8,128)(2,1)S(1)}, bf16[8,2048]{1,0:T(8,128)(2,1)}, u32[]{:S(2)}) copy-start(bf16[8,2048]{1,0:T(8,128)(2,1)} %k_ref.1) | copy-start | bytes 98308
  3.5 0.8 %copy-start.3 = (bf16[8,2048]{1,0:T(8,128)(2,1)S(1)}, bf16[8,2048]{1,0:T(8,128)(2,1)}, u32[]{:S(2)}) copy-start(bf16[8,2048]{1,0:T(8,128)(2,1)} %v_ref.1) | copy-start | bytes 98308
  4.2 0.7 %copy-start.4 = (s32[2,32]{1,0:T(2,128)S(1)}, s32[2,32]{1,0:T(2,128)}, u32[]{:S(2)}) copy-start(s32[2,32]{1,0:T(2,128)} %mask_ref.1) | copy-start | bytes 772
  4.9 0.7 %copy-start.5 = (f32[16]{0:T(128)S(1)}, f32[16]{0:T(128)}, u32[]{:S(2)}) copy-start(f32[16]{0:T(128)} %gate_ref.1) | copy-start | bytes 196

commit v2 on v1

--- a/solution.py
+++ b/solution.py
@@ -12,14 +12,15 @@
 TQ, TM, FEAT = 128, 8, 2048
 NX, NY, NZ, NYL = 4, 8, 8, 4
 HALF = FEAT // 2
-CHUNKS = 2
+CHUNKS = 4
 CH_HEADS = HEADS // 2 // CHUNKS
 CW = CH_HEADS * HEAD_DIM
 CHIPS = NX * NYL
 ROWS = 2 * TM
 MEM = CHIPS * ROWS
 NQ = 2 * TQ
-SEMS = 80
+SEMS = 112
+VMEM_BYTES = 64_000_000
 BF, F32 = jnp.bfloat16, jnp.float32
 
 
@@ -38,7 +39,7 @@
 def kernel(
     q_ref, k_ref, v_ref, mask_ref, gate_ref, og_ref,
     att_out, qg_out, kg_out, vg_out, gg_out,
-    kx, vx, qa, oa, mb, bias, gath, att, qg, term, rxa, rxn, ysum, yrx, fin, gsl, send, recv, local,
+    kx, vx, mk, gt, qa, oa, mb, bias, gath, att, qg, term, rxa, rxn, ysum, yrx, fin, gsl, send, recv, local,
 ):
     dp, blk = lax.axis_index("dp"), lax.axis_index("blk")
     y_hi, z = dp // NZ, dp % NZ
@@ -83,10 +84,10 @@
     mine = pl.ds(pl.multiple_of(c * HALF, HALF), HALF)
     other = pl.ds(pl.multiple_of((1 - c) * HALF, HALF), HALF)
 
+    small = [stay(mask_ref, mk), stay(gate_ref, gt)]
     own_kv = [stay(k_ref.at[:, mine], kx.at[c]), stay(v_ref.at[:, mine], vx.at[c])]
     own_q = [stay(q_ref.at[:, mine], qa.at[0]), stay(og_ref.at[:, mine], oa.at[0])]
     mb[0] = jnp.zeros((8, 128), F32)
-    mb[0, 0:2, 0 : 2 * CHIPS] = mask_ref[...].astype(F32)
 
     barrier = pltpu.get_barrier_semaphore()
     peers = [to for stage in gate_peers for to in stage]
@@ -98,12 +99,14 @@
         remote(k_ref.at[:, other], kx.at[c], partner),
         remote(v_ref.at[:, other], vx.at[c], partner),
     ]
-    mask_in = remote(mb.at[0], mb.at[1], partner)
     q_in = [
         remote(q_ref.at[:, other], qa.at[1], partner),
         remote(og_ref.at[:, other], oa.at[1], partner),
     ]
 
+    for copy in small:
+        copy.wait()
+    mb[0, 0:2, 0 : 2 * CHIPS] = mk[...].astype(F32)
     for copy in own_kv:
         copy.wait()
     for copy in kv_in:
@@ -117,6 +120,30 @@
     y_in = [
         [remote(gath.at[j, me], gath.at[j, me], to) for to in y_near] for j in range(CHUNKS)
     ]
+
+    mask_in = remote(mb.at[0], mb.at[1], partner)
+
+    x_of = lambda d: (x + d) % NX
+    x_in, far_in = [], []
+
+    def send_x(j):
+        for copy in y_in[j]:
+            copy.wait_recv()
+        block = gath.at[j, pl.ds(x * NYL, NYL)]
+        x_in.append([remote(block, block, right), remote(block, block, left)])
+
+    def send_far(j):
+        x_in[j][0].wait_recv()
+        part = gath.at[j, pl.ds(x_of(3) * NYL, 2)]
+        first = remote(part, part, right)
+        x_in[j][1].wait_recv()
+        part = gath.at[j, pl.ds(x_of(1) * NYL + 2, 2)]
+        far_in.append([first, remote(part, part, left)])
+
+    send_x(0)
+    send_x(1)
+    send_far(0)
+    send_x(2)
 
     mask_in.wait_recv()
     rows = lax.broadcasted_iota(jnp.int32, (MEM, 128), 0) // TM
@@ -128,21 +155,9 @@
     )
     bias[...] = (nt(pick.astype(BF), spread.astype(BF)) - 1.0) * 1e30
 
-    x_of = lambda d: (x + d) % NX
-    x_in = []
-    for j in range(CHUNKS):
-        for copy in y_in[j]:
-            copy.wait_recv()
-        block = gath.at[j, pl.ds(x * NYL, NYL)]
-        x_in.append([remote(block, block, right), remote(block, block, left)])
-    far_in = []
-    for j in range(CHUNKS):
-        x_in[j][0].wait_recv()
-        part = gath.at[j, pl.ds(x_of(3) * NYL, 2)]
-        first = remote(part, part, right)
-        x_in[j][1].wait_recv()
-        part = gath.at[j, pl.ds(x_of(1) * NYL + 2, 2)]
-        far_in.append([first, remote(part, part, left)])
+    send_far(1)
+    send_x(3)
+    send_far(2)
 
     for copy in own_q:
         copy.wait()
@@ -153,7 +168,8 @@
     lane = lax.broadcasted_iota(jnp.int32, (8, 128), 1)
     gate_row = jnp.zeros((8, 128), F32)
     rx1 = []
-    for j in range(CHUNKS):
+
+    def compute(j, gate_row):
         for copy in far_in[j]:
             copy.wait_recv()
         for h in range(CH_HEADS):
@@ -161,7 +177,7 @@
             cols = slice(head * HEAD_DIM, (head + 1) * HEAD_DIM)
             kc = slice(h * HEAD_DIM, (h + 1) * HEAD_DIM)
             vc = slice(CW + h * HEAD_DIM, CW + (h + 1) * HEAD_DIM)
-            g = gate_ref[c * (HEADS // 2) + head]
+            g = gt[c * (HEADS // 2) + head]
             qh = qa[:, :, cols].reshape(NQ, HEAD_DIM)
             oh = oa[:, :, cols].reshape(NQ, HEAD_DIM)
             kh = gath[j, :, :, kc].reshape(MEM, HEAD_DIM)
@@ -183,6 +199,7 @@
             remote(term.at[j, pl.ds(x_of(2) * NYL, 2)], rxa.at[j, 0], right),
             remote(term.at[j, pl.ds(x_of(2) * NYL + 2, 2)], rxa.at[j, 1], left),
         ])
+        return gate_row
 
     rx2 = []
 
@@ -215,8 +232,6 @@
             row = row + gsl[base + i]
         return row
 
-    gate_send(0, gate_row)
-    reduce_x(0)
     ends = []
 
     def put(src, out, j):
@@ -225,14 +240,23 @@
         ends.append(remote(src.at[1, :, part], out.at[:, lo], partner))
         stayed.append(stay(src.at[0, :, part], out.at[:, lo]))
 
-    reduce_x(1)
     for j in range(CHUNKS):
-        put(att, att_out, j)
-        put(qg, qg_out, j)
-    gate_send(1, gate_take(0))
+        gate_row = compute(j, gate_row)
+        if j == 0:
+            send_far(CHUNKS - 1)
+        else:
+            put(att, att_out, j - 1)
+            put(qg, qg_out, j - 1)
+        if j == CHUNKS - 1:
+            gate_send(0, gate_row)
+        if j > 0:
+            reduce_x(j - 1)
+    put(att, att_out, CHUNKS - 1)
+    put(qg, qg_out, CHUNKS - 1)
 
     ry = []
-    for j in range(CHUNKS):
+
+    def reduce_y(j):
         for copy in rx2[j]:
             copy.wait_recv()
         own = term[j, pl.ds(x * NYL, NYL)].astype(F32)
@@ -241,10 +265,18 @@
             remote(ysum.at[j, (y_lo + d) % NYL], yrx.at[j, d - 1], y_near[d - 1])
             for d in range(1, NYL)
         ])
-        if j == 0:
-            gate_send(2, gate_take(1))
+
+    reduce_y(0)
+    gate_send(1, gate_take(0))
+    reduce_y(1)
+    reduce_x(CHUNKS - 1)
+    reduce_y(2)
+    gate_send(2, gate_take(1))
+    reduce_y(3)
 
     for j in range(CHUNKS):
+        if j == CHUNKS - 1:
+            gate_send(3, gate_take(2))
         for copy in ry[j]:
             copy.wait_recv()
         whole = ysum[j, y_lo].astype(F32)
@@ -256,7 +288,6 @@
             ends.append(remote(fin.at[j, 1 - c, :, part], out.at[:, lo], partner))
             stayed.append(stay(fin.at[j, c, :, part], out.at[:, lo]))
 
-    gate_send(3, gate_take(2))
     row = gate_take(3)
     gg_out[...] = row * (1.0 / math.sqrt(TQ * 512 * HEAD_DIM))
 
@@ -268,11 +299,30 @@
         copy.wait_send()
 
 
+def place(a, b, d, e, g, a_out, b_out, d_out, e_out, g_out, a_buf, b_buf, d_buf, e_buf, g_buf, sems):
+    staged = [(a, a_buf, a_out), (b, b_buf, b_out), (d, d_buf, d_out), (e, e_buf, e_out)]
+    taken = [
+        pltpu.make_async_copy(src, buf, sems.at[i]) for i, (src, buf, _) in enumerate(staged)
+    ] + [pltpu.make_async_copy(g, g_buf, sems.at[4])]
+    put = [
+        pltpu.make_async_copy(buf, dst, sems.at[5 + i]) for i, (_, buf, dst) in enumerate(staged)
+    ]
+    for copy in taken:
+        copy.start()
+    for into, out in zip(taken, put):
+        into.wait()
+        out.start()
+    taken[4].wait()
+    g_out[...] = g_buf[0, :HEADS]
+    for copy in put:
+        copy.wait()
+
+
 def on_device(queries, keys, memory_values, block_mask, head_gate, out_grad):
     anywhere = pl.BlockSpec(memory_space=pl.ANY)
+    hbm = pl.BlockSpec(memory_space=pltpu.HBM)
     vmem = pl.BlockSpec(memory_space=pltpu.VMEM)
-    smem = pl.BlockSpec(memory_space=pltpu.SMEM)
-    attended, query_gradient, key_gradient, value_gradient, gate = pl.pallas_call(
+    results = pl.pallas_call(
         kernel,
         out_shape=(
             jax.ShapeDtypeStruct((TQ, FEAT), BF),
@@ -281,11 +331,13 @@
             jax.ShapeDtypeStruct((TM, FEAT), F32),
             jax.ShapeDtypeStruct((8, 128), F32),
         ),
-        in_specs=[anywhere, anywhere, anywhere, vmem, smem, anywhere],
+        in_specs=[hbm] * 6,
         out_specs=(anywhere, anywhere, anywhere, anywhere, vmem),
         scratch_shapes=[
             pltpu.VMEM((2, TM, HALF), BF),
             pltpu.VMEM((2, TM, HALF), BF),
+            pltpu.VMEM((2, 2 * CHIPS), jnp.int32),
+            pltpu.SMEM((HEADS,), F32),
             pltpu.VMEM((2, TQ, HALF), BF),
             pltpu.VMEM((2, TQ, HALF), BF),
             pltpu.VMEM((2, 8, 128), F32),
@@ -302,13 +354,33 @@
             pltpu.VMEM((NX + NY + NZ + 2, 8, 128), F32),
             pltpu.SemaphoreType.DMA((SEMS,)),
             pltpu.SemaphoreType.DMA((SEMS,)),
-            pltpu.SemaphoreType.DMA((16,)),
+            pltpu.SemaphoreType.DMA((32,)),
         ],
         compiler_params=pltpu.CompilerParams(
-            collective_id=0, has_side_effects=True, vmem_limit_bytes=40 * 1024 * 1024
+            collective_id=0, has_side_effects=True, vmem_limit_bytes=VMEM_BYTES
         ),
     )(queries, keys, memory_values, block_mask, head_gate, out_grad)
-    return attended, query_gradient, key_gradient, value_gradient, gate[0, :HEADS]
+    return pl.pallas_call(
+        place,
+        out_shape=(
+            jax.ShapeDtypeStruct((TQ, FEAT), BF),
+            jax.ShapeDtypeStruct((TQ, FEAT), BF),
+            jax.ShapeDtypeStruct((TM, FEAT), F32),
+            jax.ShapeDtypeStruct((TM, FEAT), F32),
+            jax.ShapeDtypeStruct((HEADS,), F32),
+        ),
+        in_specs=[hbm] * 5,
+        out_specs=(hbm, hbm, hbm, hbm, vmem),
+        scratch_shapes=[
+            pltpu.VMEM((TQ, FEAT), BF),
+            pltpu.VMEM((TQ, FEAT), BF),
+            pltpu.VMEM((TM, FEAT), F32),
+            pltpu.VMEM((TM, FEAT), F32),
+            pltpu.VMEM((8, 128), F32),
+            pltpu.SemaphoreType.DMA((9,)),
+        ],
+        compiler_params=pltpu.CompilerParams(vmem_limit_bytes=VMEM_BYTES),
+    )(*results)
 
 
 def solution(mesh):

time: 62.8 us -> 57.8 us (0.920)
  local copies, waits for them, and re-layouts: 8.28 us -> 0 us
  Pallas kernels: 53.5 us -> 57 us
    unnamed x16 -> x0, local copies, waits for them, and re-layouts: 7.77 us -> none
    pallas_call x0 -> x1, Pallas kernels: none -> 2.63 us  [on_device(): pl.pallas_call(place, out_shape=(jax.ShapeDtypeStruct((TQ, FEAT), BF), ja...]
    pallas_call x1, Pallas kernels: 53.5 us -> 54.4 us  [on_device(): pl.pallas_call(kernel, out_shape=(jax.ShapeDtypeStruct((TQ, FEAT), BF), j...]
where the time goes in v2:
time: 57.8 us; the launch traced here: 57.6 us
  Pallas kernels  57 us (99%)
  between operations  0.64 us (1%)
    pallas_call x1, Pallas kernels, on_device(): pl.pallas_call(kernel, out_shape=(jax.ShapeDtypeStruct((TQ, FEAT), BF), j...  54.4 us
    pallas_call x1, Pallas kernels, on_device(): pl.pallas_call(place, out_shape=(jax.ShapeDtypeStruct((TQ, FEAT), BF), ja...  2.63 us

profile of v2, /device:TPU:1, one launch (start us, length us, event | category | flops | bytes accessed | tf_op | source)
XLA Modules:
  0.0 57.6 jit_solution(10069877912111817056)
XLA Ops:
  0.6 54.4 %shard_map.101 = (bf16[128,2048]{1,0:T(8,128)(2,1)}, bf16[128,2048]{1,0:T(8,128)(2,1)}, f32[8,2048]{1,0:T(8,128)}, f32[8,2048]{1,0:T(8,128)}, f32[8,128]{1,0:T(8,128)}) custom-call(bf16[128,2048]{1,0:T(8,128)(2,1)} %q_ref.1, bf16[8,2048]{1,0:T(8,128)(2,1)} %k_ref.1, bf16[8,2048]{1,0:T(8,128)(2,1)} %v_ref.1, s32[2,32]{1,0:T(2,128)} %mask_ref.1, f32[16]{0:T(128)} %gate_ref.1, ...), custom_call_target="tpu_custom_call" | custom-call | tf_op jit(solution)/shard_map/pallas_call | solution.py:325
  55.0 2.6 %shard_map.102 = (bf16[128,2048]{1,0:T(8,128)(2,1)}, bf16[128,2048]{1,0:T(8,128)(2,1)}, f32[8,2048]{1,0:T(8,128)}, f32[8,2048]{1,0:T(8,128)}, f32[16]{0:T(128)}) custom-call(bf16[128,2048]{1,0:T(8,128)(2,1)} %get-tuple-element.10.a, bf16[128,2048]{1,0:T(8,128)(2,1)} %get-tuple-element.11.b, f32[8,2048]{1,0:T(8,128)} %get-tuple-element.12.d, ...), custom_call_target="tpu_custom_call" | custom-call | tf_op jit(solution)/shard_map/pallas_call | solution.py:363

commit v3 on v2

--- a/solution.py
+++ b/solution.py
@@ -19,7 +19,7 @@
 ROWS = 2 * TM
 MEM = CHIPS * ROWS
 NQ = 2 * TQ
-SEMS = 112
+SEMS = 144
 VMEM_BYTES = 64_000_000
 BF, F32 = jnp.bfloat16, jnp.float32
 
@@ -39,7 +39,7 @@
 def kernel(
     q_ref, k_ref, v_ref, mask_ref, gate_ref, og_ref,
     att_out, qg_out, kg_out, vg_out, gg_out,
-    kx, vx, mk, gt, qa, oa, mb, bias, gath, att, qg, term, rxa, rxn, ysum, yrx, fin, gsl, send, recv, local,
+    st, mk, gt, qa, oa, mb, bias, gath, att, qg, term, rxa, rxn, ysum, yrx, fin, gsl, send, recv, local,
 ):
     dp, blk = lax.axis_index("dp"), lax.axis_index("blk")
     y_hi, z = dp // NZ, dp % NZ
@@ -53,11 +53,12 @@
     partner = device(c=1 - c)
     right, left = device(x=(x + 1) % NX), device(x=(x + NX - 1) % NX)
     y_near = [device(y=y_hi * NYL + (y_lo + d) % NYL) for d in range(1, NYL)]
+    y_cross = [device(y=y_hi * NYL + (y_lo + d) % NYL, c=1 - c) for d in range(1, NYL)]
     gate_peers = [
-        [device(x=(x + d) % NX) for d in range(1, NX)],
+        [partner]
+        + [device(x=(x + d) % NX, c=o) for d in range(1, NX) for o in (c, 1 - c)],
         [device(y=(y + d) % NY) for d in range(1, NY)],
         [device(z=(z + d) % NZ) for d in range(1, NZ)],
-        [partner],
     ]
 
     count = [0, 0]
@@ -85,20 +86,37 @@
     other = pl.ds(pl.multiple_of((1 - c) * HALF, HALF), HALF)
 
     small = [stay(mask_ref, mk), stay(gate_ref, gt)]
-    own_kv = [stay(k_ref.at[:, mine], kx.at[c]), stay(v_ref.at[:, mine], vx.at[c])]
+    rows_in = [
+        [
+            stay(ref.at[:, h * HALF + j * CW : h * HALF + (j + 1) * CW], st.at[h, j, :, at : at + CW])
+            for h in range(2)
+            for ref, at in ((k_ref, 0), (v_ref, CW))
+        ]
+        for j in range(CHUNKS)
+    ]
     own_q = [stay(q_ref.at[:, mine], qa.at[0]), stay(og_ref.at[:, mine], oa.at[0])]
     mb[0] = jnp.zeros((8, 128), F32)
 
     barrier = pltpu.get_barrier_semaphore()
-    peers = [to for stage in gate_peers for to in stage]
+    peers = [to for stage in gate_peers for to in stage] + y_cross
     for to in peers:
         pl.semaphore_signal(barrier, inc=1, device_id=to, device_id_type=MESH)
     pl.semaphore_wait(barrier, len(peers))
 
-    kv_in = [
-        remote(k_ref.at[:, other], kx.at[c], partner),
-        remote(v_ref.at[:, other], vx.at[c], partner),
-    ]
+    def send_y(j):
+        for copy in rows_in[j]:
+            copy.wait()
+        own.append(stay(st.at[c, j], gath.at[j, me, c]))
+        taken = [remote(st.at[1 - c, j], gath.at[j, me, c], partner)]
+        for same, cross in zip(y_near, y_cross):
+            taken.append(remote(st.at[c, j], gath.at[j, me, c], same))
+            taken.append(remote(st.at[1 - c, j], gath.at[j, me, c], cross))
+        y_in.append(taken)
+
+    own, y_in = [], []
+    for j in range(CHUNKS):
+        send_y(j)
+
     q_in = [
         remote(q_ref.at[:, other], qa.at[1], partner),
         remote(og_ref.at[:, other], oa.at[1], partner),
@@ -107,26 +125,13 @@
     for copy in small:
         copy.wait()
     mb[0, 0:2, 0 : 2 * CHIPS] = mk[...].astype(F32)
-    for copy in own_kv:
-        copy.wait()
-    for copy in kv_in:
-        copy.wait_recv()
-    k_rows = kx[...].astype(F32).reshape(ROWS, HALF).astype(BF)
-    v_rows = vx[...].astype(F32).reshape(ROWS, HALF).astype(BF)
-    for j in range(CHUNKS):
-        gath[j, me, :, 0:CW] = k_rows[:, j * CW : (j + 1) * CW]
-        gath[j, me, :, CW : 2 * CW] = v_rows[:, j * CW : (j + 1) * CW]
-
-    y_in = [
-        [remote(gath.at[j, me], gath.at[j, me], to) for to in y_near] for j in range(CHUNKS)
-    ]
-
     mask_in = remote(mb.at[0], mb.at[1], partner)
 
     x_of = lambda d: (x + d) % NX
     x_in, far_in = [], []
 
     def send_x(j):
+        own[j].wait()
         for copy in y_in[j]:
             copy.wait_recv()
         block = gath.at[j, pl.ds(x * NYL, NYL)]
@@ -180,8 +185,8 @@
             g = gt[c * (HEADS // 2) + head]
             qh = qa[:, :, cols].reshape(NQ, HEAD_DIM)
             oh = oa[:, :, cols].reshape(NQ, HEAD_DIM)
-            kh = gath[j, :, :, kc].reshape(MEM, HEAD_DIM)
-            vh = gath[j, :, :, vc].reshape(MEM, HEAD_DIM)
+            kh = gath[j, :, :, :, kc].astype(F32).reshape(MEM, HEAD_DIM).astype(BF)
+            vh = gath[j, :, :, :, vc].astype(F32).reshape(MEM, HEAD_DIM).astype(BF)
             s = nt(kh, qh) * (scale * math.log2(math.e)) + bias[...]
             e = jnp.exp2(s - jnp.max(s, axis=0, keepdims=True))
             p = e * (1.0 / jnp.sum(e, axis=0, keepdims=True))
@@ -189,8 +194,8 @@
             dp_ = nt(vh, oh)
             delta = jnp.sum(low.astype(F32) * dp_, axis=0, keepdims=True)
             ds = (p * (dp_ - delta) * (g * scale)).astype(BF)
-            term[j, :, :, kc] = nn(ds, qh).astype(BF).reshape(CHIPS, ROWS, HEAD_DIM)
-            term[j, :, :, vc] = (nn(low, oh) * g).astype(BF).reshape(CHIPS, ROWS, HEAD_DIM)
+            term[j, :, :, :, kc] = nn(ds, qh).reshape(CHIPS, 2, TM, HEAD_DIM).astype(BF)
+            term[j, :, :, :, vc] = (nn(low, oh) * g).reshape(CHIPS, 2, TM, HEAD_DIM).astype(BF)
             att[:, :, cols] = (tn(low, vh) * g).astype(BF).reshape(2, TQ, HEAD_DIM)
             qg[:, :, cols] = tn(ds, kh).astype(BF).reshape(2, TQ, HEAD_DIM)
             total = jnp.sum(delta, axis=1, keepdims=True)
@@ -213,7 +218,7 @@
         term[j, to] = (term[j, to].astype(F32) + rxa[j, 1].astype(F32)).astype(BF)
         rx2.append([first, remote(term.at[j, pl.ds(x_of(3) * NYL, NYL)], rxn.at[j, 1], left)])
 
-    gate_slots = [(0, NX, x), (NX, NY, y), (NX + NY, NZ, z), (NX + NY + NZ, 2, c)]
+    gate_slots = [(0, 2 * NX, 2 * x + c), (2 * NX, NY, y), (2 * NX + NY, NZ, z)]
     gate_in = []
 
     def gate_send(stage, row):
@@ -261,10 +266,12 @@
             copy.wait_recv()
         own = term[j, pl.ds(x * NYL, NYL)].astype(F32)
         ysum[j] = (own + rxn[j, 0].astype(F32) + rxn[j, 1].astype(F32)).astype(BF)
-        ry.append([
-            remote(ysum.at[j, (y_lo + d) % NYL], yrx.at[j, d - 1], y_near[d - 1])
-            for d in range(1, NYL)
-        ])
+        taken = [remote(ysum.at[j, y_lo, 1 - c], yrx.at[j, 0, 1], partner)]
+        for d in range(1, NYL):
+            to = (y_lo + d) % NYL
+            taken.append(remote(ysum.at[j, to, c], yrx.at[j, d, 0], y_near[d - 1]))
+            taken.append(remote(ysum.at[j, to, 1 - c], yrx.at[j, d, 1], y_cross[d - 1]))
+        ry.append(taken)
 
     reduce_y(0)
     gate_send(1, gate_take(0))
@@ -275,20 +282,20 @@
     reduce_y(3)
 
     for j in range(CHUNKS):
-        if j == CHUNKS - 1:
-            gate_send(3, gate_take(2))
         for copy in ry[j]:
             copy.wait_recv()
-        whole = ysum[j, y_lo].astype(F32)
-        for d in range(NYL - 1):
-            whole = whole + yrx[j, d].astype(F32)
-        fin[j] = whole.reshape(2, TM, 2 * CW)
-        lo = pl.ds(pl.multiple_of(c * HALF + j * CW, CW), CW)
-        for out, part in ((kg_out, slice(0, CW)), (vg_out, slice(CW, 2 * CW))):
-            ends.append(remote(fin.at[j, 1 - c, :, part], out.at[:, lo], partner))
-            stayed.append(stay(fin.at[j, c, :, part], out.at[:, lo]))
-
-    row = gate_take(3)
+        same = ysum[j, y_lo, c].astype(F32)
+        cross = yrx[j, 0, 1].astype(F32)
+        for d in range(1, NYL):
+            same = same + yrx[j, d, 0].astype(F32)
+            cross = cross + yrx[j, d, 1].astype(F32)
+        for r, (half, whole) in enumerate(((c, same), (1 - c, cross))):
+            fin[j, r] = whole
+            lo = pl.ds(pl.multiple_of(half * HALF + j * CW, CW), CW)
+            for out, part in ((kg_out, slice(0, CW)), (vg_out, slice(CW, 2 * CW))):
+                stayed.append(stay(fin.at[j, r, :, part], out.at[:, lo]))
+
+    row = gate_take(2)
     gg_out[...] = row * (1.0 / math.sqrt(TQ * 512 * HEAD_DIM))
 
     for copy in ends:
@@ -334,27 +341,26 @@
         in_specs=[hbm] * 6,
         out_specs=(anywhere, anywhere, anywhere, anywhere, vmem),
         scratch_shapes=[
-            pltpu.VMEM((2, TM, HALF), BF),
-            pltpu.VMEM((2, TM, HALF), BF),
+            pltpu.VMEM((2, CHUNKS, TM, 2 * CW), BF),
             pltpu.VMEM((2, 2 * CHIPS), jnp.int32),
             pltpu.SMEM((HEADS,), F32),
             pltpu.VMEM((2, TQ, HALF), BF),
             pltpu.VMEM((2, TQ, HALF), BF),
             pltpu.VMEM((2, 8, 128), F32),
             pltpu.VMEM((MEM, NQ), F32),
-            pltpu.VMEM((CHUNKS, CHIPS, ROWS, 2 * CW), BF),
+            pltpu.VMEM((CHUNKS, CHIPS, 2, TM, 2 * CW), BF),
             pltpu.VMEM((2, TQ, HALF), BF),
             pltpu.VMEM((2, TQ, HALF), BF),
-            pltpu.VMEM((CHUNKS, CHIPS, ROWS, 2 * CW), BF),
-            pltpu.VMEM((CHUNKS, 2, 2, ROWS, 2 * CW), BF),
-            pltpu.VMEM((CHUNKS, 2, NYL, ROWS, 2 * CW), BF),
-            pltpu.VMEM((CHUNKS, NYL, ROWS, 2 * CW), BF),
-            pltpu.VMEM((CHUNKS, NYL - 1, ROWS, 2 * CW), BF),
+            pltpu.VMEM((CHUNKS, CHIPS, 2, TM, 2 * CW), BF),
+            pltpu.VMEM((CHUNKS, 2, 2, 2, TM, 2 * CW), BF),
+            pltpu.VMEM((CHUNKS, 2, NYL, 2, TM, 2 * CW), BF),
+            pltpu.VMEM((CHUNKS, NYL, 2, TM, 2 * CW), BF),
+            pltpu.VMEM((CHUNKS, NYL, 2, TM, 2 * CW), BF),
             pltpu.VMEM((CHUNKS, 2, TM, 2 * CW), F32),
-            pltpu.VMEM((NX + NY + NZ + 2, 8, 128), F32),
+            pltpu.VMEM((2 * NX + NY + NZ, 8, 128), F32),
             pltpu.SemaphoreType.DMA((SEMS,)),
             pltpu.SemaphoreType.DMA((SEMS,)),
-            pltpu.SemaphoreType.DMA((32,)),
+            pltpu.SemaphoreType.DMA((64,)),
         ],
         compiler_params=pltpu.CompilerParams(
             collective_id=0, has_side_effects=True, vmem_limit_bytes=VMEM_BYTES

time: 57.8 us -> 56.5 us (0.978)
  Pallas kernels: 57 us -> 55.7 us
    pallas_call x1, Pallas kernels: 54.4 us -> 53.1 us  [on_device(): pl.pallas_call(kernel, out_shape=(jax.ShapeDtypeStruct((TQ, FEAT), BF), j...]
where the time goes in v3:
time: 56.5 us; the launch traced here: 56.4 us
  Pallas kernels  55.7 us (99%)
  between operations  0.64 us (1%)
    pallas_call x1, Pallas kernels, on_device(): pl.pallas_call(kernel, out_shape=(jax.ShapeDtypeStruct((TQ, FEAT), BF), j...  53.1 us
    pallas_call x1, Pallas kernels, on_device(): pl.pallas_call(place, out_shape=(jax.ShapeDtypeStruct((TQ, FEAT), BF), ja...  2.63 us

profile of v3, /device:TPU:1, one launch (start us, length us, event | category | flops | bytes accessed | tf_op | source)
XLA Modules:
  0.0 56.4 jit_solution(15033732378243007214)
XLA Ops:
  0.6 53.1 %shard_map.101 = (bf16[128,2048]{1,0:T(8,128)(2,1)}, bf16[128,2048]{1,0:T(8,128)(2,1)}, f32[8,2048]{1,0:T(8,128)}, f32[8,2048]{1,0:T(8,128)}, f32[8,128]{1,0:T(8,128)}) custom-call(bf16[128,2048]{1,0:T(8,128)(2,1)} %q_ref.1, bf16[8,2048]{1,0:T(8,128)(2,1)} %k_ref.1, bf16[8,2048]{1,0:T(8,128)(2,1)} %v_ref.1, s32[2,32]{1,0:T(2,128)} %mask_ref.1, f32[16]{0:T(128)} %gate_ref.1, ...), custom_call_target="tpu_custom_call" | custom-call | tf_op jit(solution)/shard_map/pallas_call | solution.py:332
  53.7 2.6 %shard_map.102 = (bf16[128,2048]{1,0:T(8,128)(2,1)}, bf16[128,2048]{1,0:T(8,128)(2,1)}, f32[8,2048]{1,0:T(8,128)}, f32[8,2048]{1,0:T(8,128)}, f32[16]{0:T(128)}) custom-call(bf16[128,2048]{1,0:T(8,128)(2,1)} %get-tuple-element.10.a, bf16[128,2048]{1,0:T(8,128)(2,1)} %get-tuple-element.11.b, f32[8,2048]{1,0:T(8,128)} %get-tuple-element.12.d, ...), custom_call_target="tpu_custom_call" | custom-call | tf_op jit(solution)/shard_map/pallas_call | solution.py:369

commit v4 on v3

--- a/solution.py
+++ b/solution.py
@@ -107,10 +107,11 @@
         for copy in rows_in[j]:
             copy.wait()
         own.append(stay(st.at[c, j], gath.at[j, me, c]))
-        taken = [remote(st.at[1 - c, j], gath.at[j, me, c], partner)]
-        for same, cross in zip(y_near, y_cross):
-            taken.append(remote(st.at[c, j], gath.at[j, me, c], same))
-            taken.append(remote(st.at[1 - c, j], gath.at[j, me, c], cross))
+        taken = []
+        for i in (1, 2, 0):
+            taken.append(remote(st.at[c, j], gath.at[j, me, c], y_near[i]))
+            taken.append(remote(st.at[1 - c, j], gath.at[j, me, c], y_cross[i]))
+        taken.append(remote(st.at[1 - c, j], gath.at[j, me, c], partner))
         y_in.append(taken)
 
     own, y_in = [], []
@@ -267,7 +268,7 @@
         own = term[j, pl.ds(x * NYL, NYL)].astype(F32)
         ysum[j] = (own + rxn[j, 0].astype(F32) + rxn[j, 1].astype(F32)).astype(BF)
         taken = [remote(ysum.at[j, y_lo, 1 - c], yrx.at[j, 0, 1], partner)]
-        for d in range(1, NYL):
+        for d in (2, 3, 1):
             to = (y_lo + d) % NYL
             taken.append(remote(ysum.at[j, to, c], yrx.at[j, d, 0], y_near[d - 1]))
             taken.append(remote(ysum.at[j, to, 1 - c], yrx.at[j, d, 1], y_cross[d - 1]))

time: 56.5 us -> 56.4 us (level)
  no operation moved by 1% of the time
where the time goes in v4:
time: 56.4 us; the launch traced here: 56.3 us
  Pallas kernels  55.6 us (99%)
  between operations  0.64 us (1%)
    pallas_call x1, Pallas kernels, on_device(): pl.pallas_call(kernel, out_shape=(jax.ShapeDtypeStruct((TQ, FEAT), BF), j...  53 us
    pallas_call x1, Pallas kernels, on_device(): pl.pallas_call(place, out_shape=(jax.ShapeDtypeStruct((TQ, FEAT), BF), ja...  2.63 us

profile of v4, /device:TPU:1, one launch (start us, length us, event | category | flops | bytes accessed | tf_op | source)
XLA Modules:
  0.0 56.3 jit_solution(11423331406412915370)
XLA Ops:
  0.6 53.0 %shard_map.101 = (bf16[128,2048]{1,0:T(8,128)(2,1)}, bf16[128,2048]{1,0:T(8,128)(2,1)}, f32[8,2048]{1,0:T(8,128)}, f32[8,2048]{1,0:T(8,128)}, f32[8,128]{1,0:T(8,128)}) custom-call(bf16[128,2048]{1,0:T(8,128)(2,1)} %q_ref.1, bf16[8,2048]{1,0:T(8,128)(2,1)} %k_ref.1, bf16[8,2048]{1,0:T(8,128)(2,1)} %v_ref.1, s32[2,32]{1,0:T(2,128)} %mask_ref.1, f32[16]{0:T(128)} %gate_ref.1, ...), custom_call_target="tpu_custom_call" | custom-call | tf_op jit(solution)/shard_map/pallas_call | solution.py:333
  53.6 2.6 %shard_map.102 = (bf16[128,2048]{1,0:T(8,128)(2,1)}, bf16[128,2048]{1,0:T(8,128)(2,1)}, f32[8,2048]{1,0:T(8,128)}, f32[8,2048]{1,0:T(8,128)}, f32[16]{0:T(128)}) custom-call(bf16[128,2048]{1,0:T(8,128)(2,1)} %get-tuple-element.10.a, bf16[128,2048]{1,0:T(8,128)(2,1)} %get-tuple-element.11.b, f32[8,2048]{1,0:T(8,128)} %get-tuple-element.12.d, ...), custom_call_target="tpu_custom_call" | custom-call | tf_op jit(solution)/shard_map/pallas_call | solution.py:370
